TPU v7x, 256 devices: a whole 4x4x8 slice. The times are simulated.
256 devices in a mesh: feat: 4 (over y), rows: 64 (over x, z, core).
Axes of the slice: x: 4, y: 4, z: 8, core: 2. Of those that a mesh axis runs over, the one named last changes fastest.
Arguments:
- features: bfloat16 [16384, 4096], P('rows', 'feat'), may hold values from -16 to 16
- labels: int32 [16384], P('rows'), may hold values from 0 to 639
- inv_gram: float32 [4, 1024, 1024], P('feat'), may hold values from -1 to 1, as said below
Outputs:
- weights: float32 [4096, 640], P(('feat', 'rows'))
- after_block: float32 [4, 16384, 640], P('feat', 'rows')
Inputs may be any that keep to these rules, and one draw needn't show every extreme that they name: Each of the 4 matrices of inv_gram is symmetric.
All inputs are finite; a program needn't handle non-finite values.
Results may differ from a plain program's by a relative error of at most 0.0094.
Values sent between devices are 32-bit elements; how exact they have to be, the bound alone decides.
No kernel may reach another device: no remote copies, remote signals or barrier semaphores. Data moves between devices by JAX's collectives and lax.ppermute only.
A program may use at most 64 MiB of HBM per device.

v0:
```python
import jax
import jax.numpy as jnp
from jax import lax
from jax.sharding import PartitionSpec as P

C = 640
CLS_BLK = 128


def shifted(value, axis, by):
    count = lax.axis_size(axis)
    pairs = [(i, i + by) for i in range(count) if 0 <= i + by < count]
    return lax.ppermute(value, axis, pairs)


def local(features, labels, inv_gram):
    rows_here = features.shape[0]
    block_width = features.shape[1]
    group_total = lax.axis_size("feat")
    shard_total = lax.axis_size("rows")
    feat_index = lax.axis_index("feat")
    shard_index = lax.axis_index("rows")
    row_share = block_width // shard_total
    class_block = CLS_BLK
    wave_total = C // class_block
    class_ids = jnp.arange(C, dtype=jnp.int32)
    onehot = (labels[:, None] == class_ids[None, :]).astype(jnp.float32)
    counts = lax.psum(jnp.sum(onehot, axis=0), "rows")
    count_row = jnp.sum(onehot * counts[None, :], axis=1)
    row_weight = float(rows_here * shard_total) / (C * count_row)
    inverse = inv_gram[0]
    residual = jnp.where(feat_index == 0, onehot, jnp.zeros_like(onehot))
    solved_all = jnp.zeros((row_share, C), jnp.float32)
    own_first = shard_index * row_share
    for segment in range(group_total + wave_total - 1):
        wave_index = segment - feat_index
        active = (wave_index >= 0) & (wave_index < wave_total)
        column_start = jnp.clip(wave_index, 0, wave_total - 1) * class_block
        current = lax.dynamic_slice_in_dim(residual, column_start, class_block, 1)
        scaled = (row_weight[:, None] * current).astype(jnp.bfloat16)
        partial_value = lax.dot_general(
            features, scaled, (((0,), (0,)), ((), ())), preferred_element_type=jnp.float32
        )
        summed = lax.psum(partial_value, "rows")
        solved = jnp.dot(
            inverse, summed, precision=lax.Precision.HIGHEST, preferred_element_type=jnp.float32
        )
        correction = jnp.dot(
            features, solved.astype(jnp.bfloat16), preferred_element_type=jnp.float32
        )
        new_rows = lax.dynamic_slice_in_dim(solved, own_first, row_share, 0)
        updated = current - correction
        residual = jnp.where(
            active, lax.dynamic_update_slice_in_dim(residual, updated, column_start, 1), residual
        )
        solved_all = jnp.where(
            active,
            lax.dynamic_update_slice_in_dim(solved_all, new_rows, column_start, 1),
            solved_all,
        )
        arrived = shifted(updated, "feat", 1)
        incoming = segment - feat_index + 1
        landing = (feat_index >= 1) & (incoming >= 0) & (incoming < wave_total)
        landing_start = jnp.clip(incoming, 0, wave_total - 1) * class_block
        residual = jnp.where(
            landing, lax.dynamic_update_slice_in_dim(residual, arrived, landing_start, 1), residual
        )
    return (solved_all, residual[None])


def solution(mesh):
    in_specs = (P("rows", "feat"), P("rows"), P("feat", None, None))
    out_specs = (P(("feat", "rows"), None), P("feat", "rows", None))
    return jax.shard_map(local, mesh=mesh, in_specs=in_specs, out_specs=out_specs, check_vma=False)
```

profile of v0, /device:TPU:8, one launch (start us, length us, event | category | flops | bytes accessed | tf_op | source)
XLA Modules:
  0.0 1711.2 jit_solution(7271068267111447395)
XLA Ops:
  7.2 0.9 convert_reduce_fusion
  8.1 131.5 %psum.63 = f32[640]{0:T(1024)S(1)} all-reduce(f32[640]{0:T(1024)S(1)} %convert_reduce_fusion), channel_id=1, replica_groups=mesh['feat'=4,'rows'=64] {'rows'}, use_global_device_ids=true, to_apply=%region_1.0 | all-reduce | flops 640 | bytes 5120 | tf_op jit(solution)/shard_map/psum | solution.py:28
  139.7 0.9 select_reduce_fusion
  140.6 1.0 convolution_bitcast_fusion.7
  141.7 177.3 %all-reduce.9.cloned.1.call-done = f32[1024,128]{0,1:T(8,128)} async-done(((f32[1024,128]{0,1:T(8,128)}), f32[1024,128]{0,1:T(8,128)}) %all-reduce.9.cloned.1.call-update) | async-done | bytes 524304 | tf_op jit(solution)/shard_map/psum | solution.py:44
  319.0 6.7 fusion.14
  325.8 0.3 fusion.23
  326.1 3.4 collective-permute-start
  329.5 3.4 collective-permute-done
  333.0 1.0 convolution_bitcast_fusion.6
  334.1 180.6 %all-reduce.11.cloned.1.call-done = f32[1024,128]{0,1:T(8,128)} async-done(((f32[1024,128]{0,1:T(8,128)}), f32[1024,128]{0,1:T(8,128)}) %all-reduce.11.cloned.1.call-update) | async-done | bytes 524304 | tf_op jit(solution)/shard_map/psum | solution.py:44
  514.7 6.7 fusion.12
  521.4 0.3 fusion.22
  521.8 3.4 collective-permute-start.1
  525.2 3.4 collective-permute-done.1
  528.6 1.0 convolution_bitcast_fusion.5
  529.7 0.2 all-reduce.15.cloned.1.call-start
  529.9 180.4 %all-reduce.13.cloned.1.call-done = f32[1024,128]{0,1:T(8,128)} async-done(((f32[1024,128]{0,1:T(8,128)}), f32[1024,128]{0,1:T(8,128)}) %all-reduce.13.cloned.1.call-update) | async-done | bytes 524304 | tf_op jit(solution)/shard_map/psum | solution.py:44
  710.3 6.7 fusion.10
  717.1 0.3 fusion.21
  717.4 3.4 collective-permute-start.2
  720.8 3.4 collective-permute-done.2
  724.3 1.0 convolution_bitcast_fusion.4
  725.4 180.6 %all-reduce.15.cloned.1.call-done = f32[1024,128]{0,1:T(8,128)} async-done(((f32[1024,128]{0,1:T(8,128)}), f32[1024,128]{0,1:T(8,128)}) %all-reduce.15.cloned.1.call-update) | async-done | bytes 524304 | tf_op jit(solution)/shard_map/psum | solution.py:44
  905.9 6.7 fusion.8
  912.7 0.3 fusion.20
  913.0 3.4 collective-permute-start.3
  916.5 3.4 collective-permute-done.3
  919.9 1.0 convolution_bitcast_fusion.3
  921.0 180.5 %all-reduce.17.cloned.1.call-done = f32[1024,128]{0,1:T(8,128)} async-done(((f32[1024,128]{0,1:T(8,128)}), f32[1024,128]{0,1:T(8,128)}) %all-reduce.17.cloned.1.call-update) | async-done | bytes 524304 | tf_op jit(solution)/shard_map/psum | solution.py:44
  1101.6 6.7 fusion.6
  1108.3 0.3 fusion.19
  1108.7 3.4 collective-permute-start.4
  1112.1 3.4 collective-permute-done.4
  1115.6 1.1 convolution_bitcast_fusion.2
  1116.6 0.3 all-reduce.21.cloned.1.call-start
  1117.0 0.1 bitcast_dynamic-update-slice_fusion.1
  1117.1 180.2 %all-reduce.19.cloned.1.call-done = f32[1024,128]{0,1:T(8,128)} async-done(((f32[1024,128]{0,1:T(8,128)}), f32[1024,128]{0,1:T(8,128)}) %all-reduce.19.cloned.1.call-update) | async-done | bytes 524304 | tf_op jit(solution)/shard_map/psum | solution.py:44
  1297.2 6.7 fusion.4
  1304.0 0.3 fusion.18
  1304.3 3.4 collective-permute-start.5
  1307.8 3.4 collective-permute-done.5
  1311.2 1.1 convolution_bitcast_fusion.1
  1312.3 0.0 all-reduce.23.cloned.1.call-start
  1312.3 0.1 fusion.38
  1312.4 0.1 fusion.37
  1312.5 0.9 fusion.36
  1313.5 179.4 %all-reduce.21.cloned.1.call-done = f32[1024,128]{0,1:T(8,128)} async-done(((f32[1024,128]{0,1:T(8,128)}), f32[1024,128]{0,1:T(8,128)}) %all-reduce.21.cloned.1.call-update) | async-done | bytes 524304 | tf_op jit(solution)/shard_map/psum | solution.py:44
  1492.9 6.7 fusion.2
  1499.6 0.3 fusion.17
  1499.9 3.4 collective-permute-start.6
  1503.4 3.4 collective-permute-done.6
  1506.8 1.0 convolution_bitcast_fusion
  1507.9 0.9 fusion.35
  1508.8 0.1 fusion.34
  1508.9 0.1 fusion.33
  1509.0 179.5 %all-reduce.23.cloned.1.call-done = f32[1024,128]{0,1:T(8,128)} async-done(((f32[1024,128]{0,1:T(8,128)}), f32[1024,128]{0,1:T(8,128)}) %all-reduce.23.cloned.1.call-update) | async-done | bytes 524304 | tf_op jit(solution)/shard_map/psum | solution.py:44
  1688.5 6.7 fusion
  1695.2 0.3 fusion.16
  1695.6 0.1 fusion.32
  1695.7 0.8 copy.5
  1696.4 3.4 collective-permute-start.7
  1699.9 3.4 collective-permute-done.7
  1703.3 1.1 copy.6
  (38 shorter events, 0.8 us)
Async XLA Ops:
  7.2 133.4 %copy-start = (bf16[256,1024]{1,0:T(8,128)(2,1)S(1)}, bf16[256,1024]{1,0:T(8,128)(2,1)}, u32[]{:S(2)}) copy-start(bf16[256,1024]{1,0:T(8,128)(2,1)} %param.3) | copy-start | bytes 1572868
  7.2 311.9 %all-reduce.9.cloned.1.call-start = ((), (), s32[]{:S(2)}) async-start(), calls=%async_computation | async-start | bytes 1048576 | tf_op jit(solution)/shard_map/psum | solution.py:44
  141.6 373.0 %all-reduce.11.cloned.1.call-start = ((), (), s32[]{:S(2)}) async-start(), calls=%async_computation.1 | async-start | bytes 1048576 | tf_op jit(solution)/shard_map/psum | solution.py:44
  326.1 6.9 collective-permute-start
  334.0 376.3 %all-reduce.13.cloned.1.call-start = ((), (), s32[]{:S(2)}) async-start(), calls=%async_computation.2 | async-start | bytes 1048576 | tf_op jit(solution)/shard_map/psum | solution.py:44
  521.8 6.9 collective-permute-start.1
  529.7 376.2 %all-reduce.15.cloned.1.call-start = ((), (), s32[]{:S(2)}) async-start(), calls=%async_computation.3 | async-start | bytes 1048576 | tf_op jit(solution)/shard_map/psum | solution.py:44
  717.4 6.9 collective-permute-start.2
  725.3 376.3 %all-reduce.17.cloned.1.call-start = ((), (), s32[]{:S(2)}) async-start(), calls=%async_computation.4 | async-start | bytes 1048576 | tf_op jit(solution)/shard_map/psum | solution.py:44
  912.7 7.2 copy-start.1
  913.0 6.9 collective-permute-start.3
  921.0 376.3 %all-reduce.19.cloned.1.call-start = ((), (), s32[]{:S(2)}) async-start(), calls=%async_computation.5 | async-start | bytes 1048576 | tf_op jit(solution)/shard_map/psum | solution.py:44
  1108.3 7.2 copy-start.2
  1108.7 6.9 collective-permute-start.4
  1116.6 376.2 %all-reduce.21.cloned.1.call-start = ((), (), s32[]{:S(2)}) async-start(), calls=%async_computation.6 | async-start | bytes 1048576 | tf_op jit(solution)/shard_map/psum | solution.py:44
  1304.3 6.9 collective-permute-start.5
  1312.3 376.2 %all-reduce.23.cloned.1.call-start = ((), (), s32[]{:S(2)}) async-start(), calls=%async_computation.7 | async-start | bytes 1048576 | tf_op jit(solution)/shard_map/psum | solution.py:44
  1499.9 6.9 collective-permute-start.6
  1696.4 6.8 collective-permute-start.7
Sparse Core Ops, SparseCore 0:
  141.8 177.2 all-reduce.8
  334.2 180.4 all-reduce.10
  529.8 180.4 all-reduce.12
  725.4 180.4 all-reduce.14
  921.1 180.4 all-reduce.16
  1116.8 180.4 all-reduce.18
  1312.4 180.4 all-reduce.20
  1508.0 180.4 all-reduce.22
where the time goes:
time: 1710 us
  waiting for transfers between devices  1470 us (86%)
  blocking collectives  132 us (8%)
  matrix products  64.7 us (4%)
  starting transfers between devices  27.9 us (2%)
    psum x8, waiting for transfers between devices, local(): summed = lax.psum(partial_value, 'rows')  1440 us
    psum x1, blocking collectives, local(): counts = lax.psum(jnp.sum(onehot, axis=0), 'rows')  132 us
    dot_general x8, matrix products, local(): jnp.dot(inverse, summed, precision=lax.Precision.HIGHEST, preferred_eleme...  53.9 us
  transfers between devices with their start and end apart: 16, of which 16 were waited for; matrix products, arithmetic and copies ran while one was open for 0% of the time, Pallas kernels for 0%

commit v1 on v0

--- a/solution.py
+++ b/solution.py
@@ -25,7 +25,7 @@
     wave_total = C // class_block
     class_ids = jnp.arange(C, dtype=jnp.int32)
     onehot = (labels[:, None] == class_ids[None, :]).astype(jnp.float32)
-    counts = lax.psum(jnp.sum(onehot, axis=0), "rows")
+    counts = jnp.sum(lax.all_gather(jnp.sum(onehot, axis=0), "rows"), axis=0)
     count_row = jnp.sum(onehot * counts[None, :], axis=1)
     row_weight = float(rows_here * shard_total) / (C * count_row)
     inverse = inv_gram[0]

time: 1710 us -> 1630 us (0.953)
  blocking collectives: 132 us -> 47.2 us
    psum x1 -> x0, blocking collectives: 132 us -> none  [local(): counts = lax.psum(jnp.sum(onehot, axis=0), 'rows')]
    all_gather x0 -> x1, blocking collectives: none -> 47.2 us  [local(): counts = jnp.sum(lax.all_gather(jnp.sum(onehot, axis=0), 'rows'), axis=0)]
where the time goes in v1:
time: 1630 us
  waiting for transfers between devices  1470 us (90%)
  matrix products  64.7 us (4%)
  blocking collectives  47.2 us (3%)
  starting transfers between devices  27.9 us (2%)
    psum x8, waiting for transfers between devices, local(): summed = lax.psum(partial_value, 'rows')  1440 us
    dot_general x8, matrix products, local(): jnp.dot(inverse, summed, precision=lax.Precision.HIGHEST, preferred_eleme...  53.9 us
    all_gather x1, blocking collectives, local(): counts = jnp.sum(lax.all_gather(jnp.sum(onehot, axis=0), 'rows'), axis=0)  47.2 us
  transfers between devices with their start and end apart: 16, of which 16 were waited for; matrix products, arithmetic and copies ran while one was open for 0% of the time, Pallas kernels for 0%

profile of v1, /device:TPU:8, one launch (start us, length us, event | category | flops | bytes accessed | tf_op | source)
XLA Modules:
  0.0 1630.6 jit_solution(12035348842562350987)
XLA Ops:
  7.2 0.9 convert_reduce_fusion
  8.1 47.2 %all-gather.1 = f32[64,1,640]{2,1,0:T(1,128)S(1)} all-gather(f32[1,1,640]{2,1,0:T(1,128)S(1)} %reshape.13), channel_id=2, replica_groups=mesh['feat'=4,'rows'=64] {'rows'}, dimensions={0}, use_global_device_ids=true | all-gather | bytes 166400 | tf_op jit(solution)/shard_map/all_gather | solution.py:28
  55.3 0.1 reduce_sum.28
  55.4 0.9 select_reduce_fusion
  56.3 1.0 convolution_bitcast_fusion.7
  57.5 181.0 %all-reduce.9.cloned.1.call-done = f32[1024,128]{0,1:T(8,128)} async-done(((f32[1024,128]{0,1:T(8,128)}), f32[1024,128]{0,1:T(8,128)}) %all-reduce.9.cloned.1.call-update) | async-done | bytes 524304 | tf_op jit(solution)/shard_map/psum | solution.py:44
  238.5 6.7 fusion.14
  245.2 0.3 fusion.23
  245.5 3.4 collective-permute-start
  249.0 3.4 collective-permute-done
  252.4 1.0 convolution_bitcast_fusion.6
  253.5 180.5 %all-reduce.11.cloned.1.call-done = f32[1024,128]{0,1:T(8,128)} async-done(((f32[1024,128]{0,1:T(8,128)}), f32[1024,128]{0,1:T(8,128)}) %all-reduce.11.cloned.1.call-update) | async-done | bytes 524304 | tf_op jit(solution)/shard_map/psum | solution.py:44
  434.1 6.7 fusion.12
  440.8 0.3 fusion.22
  441.1 3.4 collective-permute-start.1
  444.6 3.4 collective-permute-done.1
  448.0 1.0 convolution_bitcast_fusion.5
  449.1 0.2 all-reduce.15.cloned.1.call-start
  449.3 180.4 %all-reduce.13.cloned.1.call-done = f32[1024,128]{0,1:T(8,128)} async-done(((f32[1024,128]{0,1:T(8,128)}), f32[1024,128]{0,1:T(8,128)}) %all-reduce.13.cloned.1.call-update) | async-done | bytes 524304 | tf_op jit(solution)/shard_map/psum | solution.py:44
  629.7 6.7 fusion.10
  636.4 0.3 fusion.21
  636.8 3.4 collective-permute-start.2
  640.2 3.4 collective-permute-done.2
  643.6 1.0 convolution_bitcast_fusion.4
  644.8 180.6 %all-reduce.15.cloned.1.call-done = f32[1024,128]{0,1:T(8,128)} async-done(((f32[1024,128]{0,1:T(8,128)}), f32[1024,128]{0,1:T(8,128)}) %all-reduce.15.cloned.1.call-update) | async-done | bytes 524304 | tf_op jit(solution)/shard_map/psum | solution.py:44
  825.3 6.7 fusion.8
  832.1 0.3 fusion.20
  832.4 3.4 collective-permute-start.3
  835.9 3.4 collective-permute-done.3
  839.3 1.0 convolution_bitcast_fusion.3
  840.4 180.5 %all-reduce.17.cloned.1.call-done = f32[1024,128]{0,1:T(8,128)} async-done(((f32[1024,128]{0,1:T(8,128)}), f32[1024,128]{0,1:T(8,128)}) %all-reduce.17.cloned.1.call-update) | async-done | bytes 524304 | tf_op jit(solution)/shard_map/psum | solution.py:44
  1021.0 6.7 fusion.6
  1027.7 0.3 fusion.19
  1028.1 3.4 collective-permute-start.4
  1031.5 3.4 collective-permute-done.4
  1035.0 1.1 convolution_bitcast_fusion.2
  1036.0 0.3 all-reduce.21.cloned.1.call-start
  1036.4 0.1 bitcast_dynamic-update-slice_fusion.1
  1036.5 180.2 %all-reduce.19.cloned.1.call-done = f32[1024,128]{0,1:T(8,128)} async-done(((f32[1024,128]{0,1:T(8,128)}), f32[1024,128]{0,1:T(8,128)}) %all-reduce.19.cloned.1.call-update) | async-done | bytes 524304 | tf_op jit(solution)/shard_map/psum | solution.py:44
  1216.6 6.7 fusion.4
  1223.4 0.3 fusion.18
  1223.7 3.4 collective-permute-start.5
  1227.1 3.4 collective-permute-done.5
  1230.6 1.1 convolution_bitcast_fusion.1
  1231.7 0.1 fusion.38
  1231.8 0.1 fusion.37
  1231.9 0.9 fusion.36
  1232.8 179.4 %all-reduce.21.cloned.1.call-done = f32[1024,128]{0,1:T(8,128)} async-done(((f32[1024,128]{0,1:T(8,128)}), f32[1024,128]{0,1:T(8,128)}) %all-reduce.21.cloned.1.call-update) | async-done | bytes 524304 | tf_op jit(solution)/shard_map/psum | solution.py:44
  1412.3 6.7 fusion.2
  1419.0 0.3 fusion.17
  1419.3 3.4 collective-permute-start.6
  1422.8 3.4 collective-permute-done.6
  1426.2 1.0 convolution_bitcast_fusion
  1427.3 0.9 fusion.35
  1428.2 0.1 fusion.34
  1428.3 0.1 fusion.33
  1428.4 179.5 %all-reduce.23.cloned.1.call-done = f32[1024,128]{0,1:T(8,128)} async-done(((f32[1024,128]{0,1:T(8,128)}), f32[1024,128]{0,1:T(8,128)}) %all-reduce.23.cloned.1.call-update) | async-done | bytes 524304 | tf_op jit(solution)/shard_map/psum | solution.py:44
  1607.9 6.7 fusion
  1614.6 0.3 fusion.16
  1615.0 0.1 fusion.32
  1615.1 0.8 copy.7
  1615.8 3.4 collective-permute-start.7
  1619.3 3.4 collective-permute-done.7
  1622.7 1.1 copy.8
  (40 shorter events, 0.8 us)
Async XLA Ops:
  7.2 49.2 %copy-start = (bf16[256,1024]{1,0:T(8,128)(2,1)S(1)}, bf16[256,1024]{1,0:T(8,128)(2,1)}, u32[]{:S(2)}) copy-start(bf16[256,1024]{1,0:T(8,128)(2,1)} %param.3) | copy-start | bytes 1572868
  7.2 231.3 %all-reduce.9.cloned.1.call-start = ((), (), s32[]{:S(2)}) async-start(), calls=%async_computation | async-start | bytes 1048576 | tf_op jit(solution)/shard_map/psum | solution.py:44
  57.4 376.7 %all-reduce.11.cloned.1.call-start = ((), (), s32[]{:S(2)}) async-start(), calls=%async_computation.1 | async-start | bytes 1048576 | tf_op jit(solution)/shard_map/psum | solution.py:44
  245.5 6.9 collective-permute-start
  253.5 376.2 %all-reduce.13.cloned.1.call-start = ((), (), s32[]{:S(2)}) async-start(), calls=%async_computation.2 | async-start | bytes 1048576 | tf_op jit(solution)/shard_map/psum | solution.py:44
  441.1 6.9 collective-permute-start.1
  449.1 376.2 %all-reduce.15.cloned.1.call-start = ((), (), s32[]{:S(2)}) async-start(), calls=%async_computation.3 | async-start | bytes 1048576 | tf_op jit(solution)/shard_map/psum | solution.py:44
  636.8 6.9 collective-permute-start.2
  644.7 376.3 %all-reduce.17.cloned.1.call-start = ((), (), s32[]{:S(2)}) async-start(), calls=%async_computation.4 | async-start | bytes 1048576 | tf_op jit(solution)/shard_map/psum | solution.py:44
  832.1 7.2 copy-start.1
  832.4 6.9 collective-permute-start.3
  840.4 376.3 %all-reduce.19.cloned.1.call-start = ((), (), s32[]{:S(2)}) async-start(), calls=%async_computation.5 | async-start | bytes 1048576 | tf_op jit(solution)/shard_map/psum | solution.py:44
  1027.7 7.2 copy-start.2
  1028.1 6.9 collective-permute-start.4
  1036.0 376.2 %all-reduce.21.cloned.1.call-start = ((), (), s32[]{:S(2)}) async-start(), calls=%async_computation.6 | async-start | bytes 1048576 | tf_op jit(solution)/shard_map/psum | solution.py:44
  1223.7 6.9 collective-permute-start.5
  1231.7 376.2 %all-reduce.23.cloned.1.call-start = ((), (), s32[]{:S(2)}) async-start(), calls=%async_computation.7 | async-start | bytes 1048576 | tf_op jit(solution)/shard_map/psum | solution.py:44
  1419.3 6.9 collective-permute-start.6
  1615.8 6.8 collective-permute-start.7
Sparse Core Ops, SparseCore 0:
  57.5 180.8 all-reduce.8
  253.6 180.4 all-reduce.10
  449.2 180.4 all-reduce.12
  644.8 180.4 all-reduce.14
  840.5 180.4 all-reduce.16
  1036.1 180.4 all-reduce.18
  1231.8 180.4 all-reduce.20
  1427.4 180.4 all-reduce.22
